TPU v7x, 32 devices: a whole 2x2x4 slice. The times are simulated.
32 devices in a mesh: ind: 4 (over x, core), mark: 4 (over z), chip: 2 (over y).
Axes of the slice: x: 2, y: 2, z: 4, core: 2. Of those that a mesh axis runs over, the one named last changes fastest.
Arguments:
- genotypes: bfloat16 [8192, 8192], P(('ind', 'chip'), 'mark'), may hold values from -0.1875 to 0.1875
- residual: float32 [8192, 1024], P(('ind', 'chip'), 'mark'), as said below
- posterior_inverse: bfloat16 [8, 1024, 1024], P('mark'), as said below
- gibbs_noise: bfloat16 [4, 8192, 256], P(None, 'mark'), may hold values from -6 to 6
- visit_order: int32 [4, 4, 2], P(None, 'mark'), may hold values from 0 to 1, each once within a row
Outputs:
- residual_after: float32 [8192, 1024], P(('ind', 'chip'), 'mark')
- effect_changes: float32 [4, 8192, 256], P(None, 'mark')
Inputs may be any that keep to these rules, and one draw needn't show every extreme that they name: `visit_order`: each row names each of the 2 marker blocks of one cycle position once. `residual`: finite real values. `posterior_inverse`: the diagonal entries are positive.
All inputs are finite; a program needn't handle non-finite values.
Results may differ from a plain program's by a relative error of at most 0.005.
Values sent between devices are 32-bit elements; how exact they have to be, the bound alone decides.
A program may use at most 128 MiB of HBM per device.

v0:
```python
import jax
import jax.numpy as jnp
from jax import lax
from jax.sharding import PartitionSpec as P

epsilon = 1e-05


def from_behind(array, axis, by):
    peers = lax.axis_size(axis)
    return lax.ppermute(array, axis, [(i, (i + by) % peers) for i in range(peers)])


def posterior_step(inverse, scores, total_sq, noise_rows, count):
    spread = total_sq / count
    scaled = (scores / count).astype(jnp.bfloat16)
    mean_part = jnp.dot(inverse, scaled, preferred_element_type=jnp.float32)
    diag_part = jnp.diagonal(inverse).astype(jnp.float32)
    return (
        mean_part + jnp.sqrt(diag_part[:, None] * (spread[None, :] + epsilon) / count) * noise_rows
    )


def local(genotypes, residual, posterior_inverse, gibbs_noise, visit_order):
    cycle_size = lax.axis_size("mark")
    groups = lax.axis_size("ind") * lax.axis_size("chip")
    count = genotypes.shape[0] * groups
    width = residual.shape[1]
    block_len = posterior_inverse.shape[1]
    blocks_here = posterior_inverse.shape[0]
    current = residual
    change_list = []
    for stop_idx in range(cycle_size):
        stop_changes = jnp.zeros((blocks_here * block_len, width), jnp.float32)
        for visit_pos in range(blocks_here):
            local_blk = visit_order[stop_idx, 0, visit_pos]
            columns = lax.dynamic_slice_in_dim(genotypes, local_blk * block_len, block_len, 1)
            sq_part = jnp.sum(current * current, axis=0)
            inverse = lax.dynamic_index_in_dim(posterior_inverse, local_blk, 0, keepdims=False)
            noise_rows = lax.slice_in_dim(
                gibbs_noise[stop_idx], visit_pos * block_len, (visit_pos + 1) * block_len, axis=0
            ).astype(jnp.float32)
            current_low = current.astype(jnp.bfloat16)
            partial_value = lax.dot_general(
                columns, current_low, (((0,), (0,)), ((), ())), preferred_element_type=jnp.float32
            )
            scores, total_sq = lax.psum((partial_value, sq_part), ("ind", "chip"))
            change = posterior_step(inverse, scores, total_sq, noise_rows, count)
            stop_changes = lax.dynamic_update_slice_in_dim(
                stop_changes, change, local_blk * block_len, 0
            )
            current = current - jnp.dot(
                columns, change.astype(jnp.bfloat16), preferred_element_type=jnp.float32
            )
        change_list.append(stop_changes)
        current = from_behind(current, "mark", 1)
    return (current, jnp.stack(change_list))


def solution(mesh):
    in_specs = (
        P(("ind", "chip"), "mark"),
        P(("ind", "chip"), "mark"),
        P("mark", None, None),
        P(None, "mark", None),
        P(None, "mark", None),
    )
    out_specs = (P(("ind", "chip"), "mark"), P(None, "mark", None))
    return jax.shard_map(local, mesh=mesh, in_specs=in_specs, out_specs=out_specs, check_vma=False)
```

profile of v0, /device:TPU:0, one launch (start us, length us, event | category | flops | bytes accessed | tf_op | source)
XLA Modules:
  0.0 635.5 jit_solution(9045469736230866958)
XLA Ops:
  40.4 16.4 %gather_fusion = bf16[1024]{0:T(1024)(128)(2,1)S(1)} fusion(bf16[1024,1024]{1,0:T(8,128)(2,1)} %get-tuple-element.8, s32[1024]{0:T(1024)S(1)} %bitcast.81), kind=kCustom, calls=%fused_computation | custom fusion | bytes 12288 | tf_op jit(solution)/shard_map/jit(diagonal)/cond/branch_0_fun/gather | solution.py:18
  57.0 15.5 %psum.113 = f32[256]{0:T(256)S(1)} all-reduce(f32[256]{0:T(256)S(1)} %multiply_reduce_fusion.7), channel_id=1, replica_groups=mesh['ind'=4,'mark'=4,'chip'=2] {'ind','chip'}, use_global_device_ids=true, to_apply=%region_2.3 | all-reduce | flops 256 | bytes 2048 | tf_op jit(solution)/shard_map/psum | solution.py:47
  80.2 16.0 %gather_fusion.1 = bf16[1024]{0:T(1024)(128)(2,1)S(1)} fusion(bf16[1024,1024]{1,0:T(8,128)(2,1)} %get-tuple-element.7, s32[1024]{0:T(1024)S(1)} %bitcast.82), kind=kCustom, calls=%fused_computation.1 | custom fusion | bytes 12288 | tf_op jit(solution)/shard_map/jit(diagonal)/cond/branch_0_fun/gather | solution.py:18
  108.4 28.1 %all-reduce.11.cloned.1.call-done = f32[1024,256]{1,0:T(8,128)} async-done(((f32[1024,256]{1,0:T(8,128)}), f32[1024,256]{1,0:T(8,128)}) %all-reduce.11.cloned.1.call-update) | async-done | bytes 1048592 | tf_op jit(solution)/shard_map/psum | solution.py:47
  144.5 23.9 %collective-permute-done = f32[1024,256]{1,0:T(8,128)S(1)} collective-permute-done((f32[1024,256]{1,0:T(8,128)}, f32[1024,256]{1,0:T(8,128)S(1)}, u32[]{:S(2)}, u32[]{:S(2)}) %collective-permute-start) | collective-permute-done | bytes 1048608 | tf_op jit(solution)/shard_map/ppermute | solution.py:11
  172.8 16.1 %gather_fusion.2 = bf16[1024]{0:T(1024)(128)(2,1)S(1)} fusion(bf16[1024,1024]{1,0:T(8,128)(2,1)} %get-tuple-element.6, s32[1024]{0:T(1024)S(1)} %bitcast.83), kind=kCustom, calls=%fused_computation.2 | custom fusion | bytes 12288 | tf_op jit(solution)/shard_map/jit(diagonal)/cond/branch_0_fun/gather | solution.py:18
  189.0 12.6 %psum.117 = f32[256]{0:T(256)S(1)} all-reduce(f32[256]{0:T(256)S(1)} %multiply_reduce_fusion.5), channel_id=1, replica_groups=mesh['ind'=4,'mark'=4,'chip'=2] {'ind','chip'}, use_global_device_ids=true, to_apply=%region_8.9 | all-reduce | flops 256 | bytes 2048 | tf_op jit(solution)/shard_map/psum | solution.py:47
  201.6 25.2 %all-reduce.13.cloned.1.call-done = f32[1024,256]{1,0:T(8,128)} async-done(((f32[1024,256]{1,0:T(8,128)}), f32[1024,256]{1,0:T(8,128)}) %all-reduce.13.cloned.1.call-update) | async-done | bytes 1048592 | tf_op jit(solution)/shard_map/psum | solution.py:47
  234.2 16.2 %gather_fusion.3 = bf16[1024]{0:T(1024)(128)(2,1)S(1)} fusion(bf16[1024,1024]{1,0:T(8,128)(2,1)} %get-tuple-element.5, s32[1024]{0:T(1024)S(1)} %bitcast.84), kind=kCustom, calls=%fused_computation.3 | custom fusion | bytes 12288 | tf_op jit(solution)/shard_map/jit(diagonal)/cond/branch_0_fun/gather | solution.py:18
  250.3 12.5 %psum.119 = f32[256]{0:T(256)S(1)} all-reduce(f32[256]{0:T(256)S(1)} %get-tuple-element.20), channel_id=1, replica_groups=mesh['ind'=4,'mark'=4,'chip'=2] {'ind','chip'}, use_global_device_ids=true, to_apply=%region_11.12 | all-reduce | flops 256 | bytes 2048 | tf_op jit(solution)/shard_map/psum | solution.py:47
  262.9 27.4 %all-reduce.15.cloned.1.call-done = f32[1024,256]{1,0:T(8,128)} async-done(((f32[1024,256]{1,0:T(8,128)}), f32[1024,256]{1,0:T(8,128)}) %all-reduce.15.cloned.1.call-update) | async-done | bytes 1048592 | tf_op jit(solution)/shard_map/psum | solution.py:47
  298.2 24.0 %collective-permute-done.1 = f32[1024,256]{1,0:T(8,128)S(1)} collective-permute-done((f32[1024,256]{1,0:T(8,128)}, f32[1024,256]{1,0:T(8,128)S(1)}, u32[]{:S(2)}, u32[]{:S(2)}) %collective-permute-start.1) | collective-permute-done | bytes 1048608 | tf_op jit(solution)/shard_map/ppermute | solution.py:11
  326.5 16.2 %gather_fusion.4 = bf16[1024]{0:T(1024)(128)(2,1)S(1)} fusion(bf16[1024,1024]{1,0:T(8,128)(2,1)} %get-tuple-element.4, s32[1024]{0:T(1024)S(1)} %bitcast.85), kind=kCustom, calls=%fused_computation.4 | custom fusion | bytes 12288 | tf_op jit(solution)/shard_map/jit(diagonal)/cond/branch_0_fun/gather | solution.py:18
  355.4 25.2 %all-reduce.17.cloned.1.call-done = f32[1024,256]{1,0:T(8,128)} async-done(((f32[1024,256]{1,0:T(8,128)}), f32[1024,256]{1,0:T(8,128)}) %all-reduce.17.cloned.1.call-update) | async-done | bytes 1048592 | tf_op jit(solution)/shard_map/psum | solution.py:47
  388.0 15.8 %gather_fusion.5 = bf16[1024]{0:T(1024)(128)(2,1)S(1)} fusion(bf16[1024,1024]{1,0:T(8,128)(2,1)} %get-tuple-element.3, s32[1024]{0:T(1024)S(1)} %bitcast.86), kind=kCustom, calls=%fused_computation.5 | custom fusion | bytes 12288 | tf_op jit(solution)/shard_map/jit(diagonal)/cond/branch_0_fun/gather | solution.py:18
  403.8 12.5 %psum.123 = f32[256]{0:T(256)S(1)} all-reduce(f32[256]{0:T(256)S(1)} %get-tuple-element.22), channel_id=1, replica_groups=mesh['ind'=4,'mark'=4,'chip'=2] {'ind','chip'}, use_global_device_ids=true, to_apply=%region_17.18 | all-reduce | flops 256 | bytes 2048 | tf_op jit(solution)/shard_map/psum | solution.py:47
  416.3 27.7 %all-reduce.19.cloned.1.call-done = f32[1024,256]{1,0:T(8,128)} async-done(((f32[1024,256]{1,0:T(8,128)}), f32[1024,256]{1,0:T(8,128)}) %all-reduce.19.cloned.1.call-update) | async-done | bytes 1048592 | tf_op jit(solution)/shard_map/psum | solution.py:47
  451.9 24.0 %collective-permute-done.2 = f32[1024,256]{1,0:T(8,128)S(1)} collective-permute-done((f32[1024,256]{1,0:T(8,128)}, f32[1024,256]{1,0:T(8,128)S(1)}, u32[]{:S(2)}, u32[]{:S(2)}) %collective-permute-start.2) | collective-permute-done | bytes 1048608 | tf_op jit(solution)/shard_map/ppermute | solution.py:11
  480.3 16.0 %gather_fusion.6 = bf16[1024]{0:T(1024)(128)(2,1)S(1)} fusion(bf16[1024,1024]{1,0:T(8,128)(2,1)} %get-tuple-element.9, s32[1024]{0:T(1024)S(1)} %bitcast.87), kind=kCustom, calls=%fused_computation.6 | custom fusion | bytes 12288 | tf_op jit(solution)/shard_map/jit(diagonal)/cond/branch_0_fun/gather | solution.py:18
  496.4 12.4 %psum.125 = f32[256]{0:T(256)S(1)} all-reduce(f32[256]{0:T(256)S(1)} %multiply_reduce_fusion.1), channel_id=1, replica_groups=mesh['ind'=4,'mark'=4,'chip'=2] {'ind','chip'}, use_global_device_ids=true, to_apply=%region_20.21 | all-reduce | flops 256 | bytes 2048 | tf_op jit(solution)/shard_map/psum | solution.py:47
  508.9 25.4 %all-reduce.21.cloned.1.call-done = f32[1024,256]{1,0:T(8,128)} async-done(((f32[1024,256]{1,0:T(8,128)}), f32[1024,256]{1,0:T(8,128)}) %all-reduce.21.cloned.1.call-update) | async-done | bytes 1048592 | tf_op jit(solution)/shard_map/psum | solution.py:47
  550.7 12.5 %psum.127 = f32[256]{0:T(256)S(1)} all-reduce(f32[256]{0:T(256)S(1)} %get-tuple-element.24), channel_id=1, replica_groups=mesh['ind'=4,'mark'=4,'chip'=2] {'ind','chip'}, use_global_device_ids=true, to_apply=%region_23.24 | all-reduce | flops 256 | bytes 2048 | tf_op jit(solution)/shard_map/psum | solution.py:47
  563.2 34.4 %all-reduce.23.cloned.1.call-done = f32[1024,256]{1,0:T(8,128)} async-done(((f32[1024,256]{1,0:T(8,128)}), f32[1024,256]{1,0:T(8,128)}) %all-reduce.23.cloned.1.call-update) | async-done | bytes 1048592 | tf_op jit(solution)/shard_map/psum | solution.py:47
  608.7 19.1 %collective-permute-done.3 = f32[1024,256]{1,0:T(8,128)S(1)} collective-permute-done((f32[1024,256]{1,0:T(8,128)S(1)}, f32[1024,256]{1,0:T(8,128)S(1)}, u32[]{:S(2)}, u32[]{:S(2)}) %collective-permute-start.3) | collective-permute-done | bytes 1048608 | tf_op jit(solution)/shard_map/ppermute | solution.py:11
  (129 shorter events, 126.5 us)
Async XLA Ops:
  7.2 65.7 %all-reduce.9.cloned.1.call-start = ((), (), s32[]{:S(2)}) async-start(), calls=%async_computation | async-start | bytes 2097152 | tf_op jit(solution)/shard_map/psum | solution.py:47
  13.1 123.5 %all-reduce.11.cloned.1.call-start = ((), (), s32[]{:S(2)}) async-start(), calls=%async_computation.1 | async-start | bytes 2097152 | tf_op jit(solution)/shard_map/psum | solution.py:47
  39.7 17.2 %copy-start.18 = (f32[1024,256]{1,0:T(8,128)S(1)}, f32[1024,256]{1,0:T(8,128)}, u32[]{:S(2)}) copy-start(f32[1024,256]{1,0:T(8,128)} %param.6) | copy-start | bytes 3145732
  74.5 3.0 copy-start.19
  80.2 146.7 %all-reduce.13.cloned.1.call-start = ((), (), s32[]{:S(2)}) async-start(), calls=%async_computation.2 | async-start | bytes 2097152 | tf_op jit(solution)/shard_map/psum | solution.py:47
  136.6 4.1 copy-start.1
  142.4 26.0 %collective-permute-start = (f32[1024,256]{1,0:T(8,128)}, f32[1024,256]{1,0:T(8,128)S(1)}, u32[]{:S(2)}, u32[]{:S(2)}) collective-permute-start(f32[1024,256]{1,0:T(8,128)} %fusion.35), channel_id=1, source_target_pairs={{0,2},{2,4},{4,6},{6,0},{1,3},{3,5},{5,7},{7,1},{8,10},{10,12},{12... | collective-permute-start | bytes 3145736 | tf_op jit(solution)/shard_map/ppermute | solution.py:11
  168.5 20.4 %copy-start.22 = (f32[1024,256]{1,0:T(8,128)}, f32[1024,256]{1,0:T(8,128)S(1)}, u32[]{:S(2)}) copy-start(f32[1024,256]{1,0:T(8,128)S(1)} %collective-permute-done) | copy-start | bytes 3145732
  172.2 118.1 %all-reduce.15.cloned.1.call-start = ((), (), s32[]{:S(2)}) async-start(), calls=%async_computation.3 | async-start | bytes 2097152 | tf_op jit(solution)/shard_map/psum | solution.py:47
  228.4 3.0 copy-start.23
  234.1 146.4 %all-reduce.17.cloned.1.call-start = ((), (), s32[]{:S(2)}) async-start(), calls=%async_computation.4 | async-start | bytes 2097152 | tf_op jit(solution)/shard_map/psum | solution.py:47
  290.3 4.1 copy-start.3
  296.1 26.0 %collective-permute-start.1 = (f32[1024,256]{1,0:T(8,128)}, f32[1024,256]{1,0:T(8,128)S(1)}, u32[]{:S(2)}, u32[]{:S(2)}) collective-permute-start(f32[1024,256]{1,0:T(8,128)} %fusion.41), channel_id=1, source_target_pairs={{0,2},{2,4},{4,6},{6,0},{1,3},{3,5},{5,7},{7,1},{8,10},{10,12},{12... | collective-permute-start | bytes 3145736 | tf_op jit(solution)/shard_map/ppermute | solution.py:11
  322.1 20.7 %copy-start.24 = (f32[1024,256]{1,0:T(8,128)}, f32[1024,256]{1,0:T(8,128)S(1)}, u32[]{:S(2)}) copy-start(f32[1024,256]{1,0:T(8,128)S(1)} %collective-permute-done.1) | copy-start | bytes 3145732
  325.9 118.1 %all-reduce.19.cloned.1.call-start = ((), (), s32[]{:S(2)}) async-start(), calls=%async_computation.5 | async-start | bytes 2097152 | tf_op jit(solution)/shard_map/psum | solution.py:47
  382.2 3.0 copy-start.25
  387.9 146.3 %all-reduce.21.cloned.1.call-start = ((), (), s32[]{:S(2)}) async-start(), calls=%async_computation.6 | async-start | bytes 2097152 | tf_op jit(solution)/shard_map/psum | solution.py:47
  444.1 4.1 copy-start.5
  449.9 26.0 %collective-permute-start.2 = (f32[1024,256]{1,0:T(8,128)}, f32[1024,256]{1,0:T(8,128)S(1)}, u32[]{:S(2)}, u32[]{:S(2)}) collective-permute-start(f32[1024,256]{1,0:T(8,128)} %fusion.47), channel_id=1, source_target_pairs={{0,2},{2,4},{4,6},{6,0},{1,3},{3,5},{5,7},{7,1},{8,10},{10,12},{12... | collective-permute-start | bytes 3145736 | tf_op jit(solution)/shard_map/ppermute | solution.py:11
  475.9 20.4 %copy-start.20 = (f32[1024,256]{1,0:T(8,128)}, f32[1024,256]{1,0:T(8,128)S(1)}, u32[]{:S(2)}) copy-start(f32[1024,256]{1,0:T(8,128)S(1)} %collective-permute-done.2) | copy-start | bytes 3145732
  479.7 118.0 %all-reduce.23.cloned.1.call-start = ((), (), s32[]{:S(2)}) async-start(), calls=%async_computation.7 | async-start | bytes 2097152 | tf_op jit(solution)/shard_map/psum | solution.py:47
  535.8 3.0 copy-start.21
  597.6 3.5 copy-start.7
  601.9 25.9 %collective-permute-start.3 = (f32[1024,256]{1,0:T(8,128)S(1)}, f32[1024,256]{1,0:T(8,128)S(1)}, u32[]{:S(2)}, u32[]{:S(2)}) collective-permute-start(f32[1024,256]{1,0:T(8,128)S(1)} %fusion.53), channel_id=1, source_target_pairs={{0,2},{2,4},{4,6},{6,0},{1,3},{3,5},{5,7},{7,1},{8,10},{10,12},{12... | collective-permute-start | bytes 3145736 | tf_op jit(solution)/shard_map/ppermute | solution.py:11
  (14 other events, 26.8 us)
Sparse Core Ops, SparseCore 0:
  13.2 59.6 all-reduce.8
  80.3 56.2 all-reduce.10
  172.3 54.4 all-reduce.12
  234.2 55.9 all-reduce.14
  326.0 54.4 all-reduce.16
  388.0 55.9 all-reduce.18
  479.8 54.4 all-reduce.20
  541.6 55.9 all-reduce.22
where the time goes:
time: 639 us; the launch traced here: 636 us
  waiting for transfers between devices  285 us (45%)
  local copies, waits for them, and re-layouts  145 us (23%)
  blocking collectives  103 us (16%)
  matrix products  56.6 us (9%)
  between operations  33.9 us (5%)
    psum x8, waiting for transfers between devices, local(): scores, total_sq = lax.psum((partial_value, sq_part), ('ind', 'chip'))  194 us
    gather x8, local copies, waits for them, and re-layouts, posterior_step(): diag_part = jnp.diagonal(inverse).astype(jnp.float32)  122 us
    psum x8, blocking collectives, local(): scores, total_sq = lax.psum((partial_value, sq_part), ('ind', 'chip'))  103 us
    ppermute x4, waiting for transfers between devices, from_behind(): lax.ppermute(array, axis, [(i, (i + by) % peers) for i in range(peers)])  91 us
    dot_general x8, matrix products, posterior_step(): mean_part = jnp.dot(inverse, scaled, preferred_element_type=jnp.float32)  26.1 us
    dot_general x8, matrix products, local(): lax.dot_general(columns, current_low, (((0,), (0,)), ((), ())), preferred...  21.8 us
  transfers between devices with their start and end apart: 12, of which 12 were waited for; matrix products, arithmetic and copies ran while one was open for 22% of the time, Pallas kernels for 0%

commit v1 on v0

v1 whole, which is shorter than its diff:
```python
import functools

import jax
import jax.numpy as jnp
from jax import lax
from jax.experimental import pallas as pl
from jax.experimental.pallas import tpu as pltpu
from jax.sharding import PartitionSpec as P

epsilon = 1e-05
MESH = pl.DeviceIdType.MESH
CHUNKS = 4
NT = (((1,), (1,)), ((), ()))


def kernel(
    cfg,
    order_ref,
    geno_ref,
    resid_ref,
    inv_ref,
    droot_ref,
    noise_ref,
    after_ref,
    change_ref,
    ebuf,
    part,
    r1,
    r2,
    full,
    scaled,
    stash,
    p1s,
    p1r,
    p2s,
    p2r,
    p3s,
    p3r,
    p4s,
    zs,
    zr,
):
    n_ind, n_mark, n_chip, chunks, stops, count, block, rows, lanes, sq_rows = cfg
    quads = n_ind // 2 * n_chip
    tc = ebuf.shape[2]
    lane_blocks = block // lanes
    sq_groups = tc // sq_rows
    ind = lax.axis_index("ind")
    mark = lax.axis_index("mark")
    y = lax.axis_index("chip")
    core = lax.rem(ind, 2)
    other = 1 - core
    q = lax.div(ind, 2) * n_chip + y
    partner = {"ind": ind + 1 - 2 * core}
    nxt = {"mark": lax.rem(mark + 1, n_mark)}
    prv = {"mark": lax.rem(mark + n_mark - 1, n_mark)}

    def chip_at(r):
        qq = lax.rem(q + r, quads)
        return qq, {"ind": lax.div(qq, n_chip) * 2 + core, "chip": lax.rem(qq, n_chip)}

    barrier = pltpu.get_barrier_semaphore()
    pl.semaphore_signal(barrier, inc=1, device_id=partner, device_id_type=MESH)
    pl.semaphore_signal(barrier, inc=1, device_id=nxt, device_id_type=MESH)
    pl.semaphore_signal(barrier, inc=1, device_id=prv, device_id_type=MESH)
    for r in range(1, quads):
        pl.semaphore_signal(barrier, inc=1, device_id=chip_at(r)[1], device_id_type=MESH)

    for c in range(chunks):
        ebuf[0, c] = resid_ref[c]
    pl.semaphore_wait(barrier, quads + 2)

    def copy(src, dst, ssem, rsem, dev):
        return pltpu.make_async_remote_copy(
            src_ref=src, dst_ref=dst, send_sem=ssem, recv_sem=rsem, device_id=dev, device_id_type=MESH
        )

    def hop(stop, c):
        return copy(ebuf.at[stop, c], ebuf.at[stop + 1, c], zs.at[stop, c], zr.at[stop, c], nxt)

    def pair(c):
        return copy(part.at[c, other], r1.at[c], p1s.at[c], p1r.at[c], partner)

    def spread_out(c, r):
        qq, dev = chip_at(r)
        return copy(part.at[c, core, qq], r2.at[c, q], p2s.at[c, qq], p2r.at[c, q], dev)

    def arrived2(c, r):
        qq, dev = chip_at(r)
        return copy(part.at[c, core, qq], r2.at[c, qq], p2s.at[c, qq], p2r.at[c, qq], dev)

    def gather(c, r):
        qq, dev = chip_at(r)
        return copy(full.at[c, core, q], full.at[c, core, q], p3s.at[c, qq], p3r.at[c, core, q], dev)

    def arrived3(c, r):
        qq, dev = chip_at(r)
        return copy(full.at[c, core, qq], full.at[c, core, qq], p3s.at[c, qq], p3r.at[c, core, qq], dev)

    def forward(c, qq):
        return copy(full.at[c, core, qq], full.at[c, core, qq], p4s.at[c, qq], p3r.at[c, core, qq], partner)

    def arrived4(c, qq):
        return copy(full.at[c, other, qq], full.at[c, other, qq], p4s.at[c, qq], p3r.at[c, other, qq], partner)

    def score(stop, j, c):
        k = order_ref[stop, 0, j]
        e = ebuf[stop, c]
        s = jnp.dot(e.astype(jnp.bfloat16), geno_ref[k], preferred_element_type=jnp.float32)
        sq = e * e
        width = sq.shape[1] // lanes
        tot = sq[:, :lanes]
        for i in range(1, width):
            tot = tot + sq[:, i * lanes : (i + 1) * lanes]
        for d in range(2 * quads):
            rg, lb = d // lane_blocks, d % lane_blocks
            sg = d % sq_groups
            part[c, d // quads, d % quads, :rows, :] = s[
                rg * rows : (rg + 1) * rows, lb * lanes : (lb + 1) * lanes
            ]
            part[c, d // quads, d % quads, rows:, :] = tot[sg * sq_rows : (sg + 1) * sq_rows]
        pair(c).start()

    def phase_a(stop, c):
        @pl.when(stop > 0)
        def _():
            hop(stop - 1, c).wait()

        score(stop, 0, c)

    def phase_b(stop, c):
        pair(c).wait()
        part[c, core] = part[c, core] + r1[c]
        for r in range(1, quads):
            spread_out(c, r).start()

    def phase_c(stop, c):
        tot = part[c, core, q]
        for r in range(1, quads):
            arrived2(c, r).wait_recv()
            tot = tot + r2[c, lax.rem(q + r, quads)]
        full[c, core, q] = tot
        for r in range(1, quads):
            gather(c, r).start()
        forward(c, q).start()
        for r in range(1, quads):
            spread_out(c, r).wait_send()

    def phase_d(stop, c):
        for r in range(1, quads):
            arrived3(c, r).wait_recv()
            forward(c, lax.rem(q + r, quads)).start()
        for r in range(1, quads):
            gather(c, r).wait_send()

    def phase_e(stop, j, c):
        for r in range(quads):
            arrived4(c, r).wait_recv()
            forward(c, r).wait_send()
        k = order_ref[stop, 0, j]
        for d in range(2 * quads):
            rg, lb = d // lane_blocks, d % lane_blocks
            scaled[rg * rows : (rg + 1) * rows, lb * lanes : (lb + 1) * lanes] = (
                full[c, d // quads, d % quads, :rows, :] * (1.0 / count)
            ).astype(jnp.bfloat16)
        sq = jnp.concatenate(
            [full[c, g // quads, g % quads, rows:, :] for g in range(sq_groups)], axis=0
        )
        spread = jnp.sum(sq, axis=1, keepdims=True) * (1.0 / count)
        root = jnp.sqrt((spread + epsilon) * (1.0 / count))
        mean = lax.dot_general(scaled[...], inv_ref[k], NT, preferred_element_type=jnp.float32)
        change = mean + (root * droot_ref[k]) * noise_ref[stop, j, c].astype(jnp.float32)
        if j == 0:
            stash[c, 0] = change
        else:
            stash[c, 1] = change
            first = order_ref[stop, 0, 0]
            change_ref[stop, 0, c] = stash[c, first]
            change_ref[stop, 1, c] = stash[c, 1 - first]
        ebuf[stop, c] = ebuf[stop, c] - lax.dot_general(
            change.astype(jnp.bfloat16), geno_ref[k], NT, preferred_element_type=jnp.float32
        )

    total = stops * chunks

    def at(x, fn):
        @pl.when(jnp.logical_and(x >= 0, x < total))
        def _():
            fn(lax.div(x, chunks), lax.rem(x, chunks))

    def last(stop, c):
        phase_e(stop, 1, c)
        hop(stop, c).start()

    def middle(stop, c):
        phase_e(stop, 0, c)
        score(stop, 1, c)

    def body(t, carry):
        at(t - 3, last)
        at(t, phase_a)
        at(t - 1, phase_d)
        at(t - 2, phase_c)
        at(t, phase_b)
        at(t - 1, middle)
        at(t - 2, phase_d)
        at(t, phase_c)
        at(t - 1, phase_b)
        return carry

    lax.fori_loop(0, total + 3, body, 0)
    for c in range(chunks):
        hop(stops - 1, c).wait()
        after_ref[c] = ebuf[stops, c]


def local(mesh_shape, genotypes, residual, posterior_inverse, gibbs_noise, visit_order):
    n_ind, n_mark, n_chip = mesh_shape
    quads = n_ind // 2 * n_chip
    people, traits = residual.shape
    count = people * n_ind * n_chip
    blocks, block = posterior_inverse.shape[:2]
    stops = gibbs_noise.shape[0]
    chunks = CHUNKS
    tc = traits // chunks
    slices = 2 * quads
    lanes = block // min(slices, block // 128)
    rows = tc * (block // lanes) // slices
    sq_rows = max(8, tc // slices)
    f32 = jnp.float32
    geno = genotypes.reshape(people, blocks, block).transpose(1, 0, 2)
    resid = residual.T.reshape(chunks, tc, people)
    noise = gibbs_noise.reshape(stops, blocks, block, traits).transpose(0, 1, 3, 2)
    noise = noise.reshape(stops, blocks, chunks, tc, block)
    droot = jnp.sqrt(jnp.diagonal(posterior_inverse, axis1=1, axis2=2).astype(f32))[:, None, :]
    cfg = (n_ind, n_mark, n_chip, chunks, stops, count, block, rows, lanes, sq_rows)
    vmem = pl.BlockSpec(memory_space=pltpu.VMEM)
    dma = pltpu.SemaphoreType.DMA
    after, changes = pl.pallas_call(
        functools.partial(kernel, cfg),
        out_shape=(
            jax.ShapeDtypeStruct((chunks, tc, people), f32),
            jax.ShapeDtypeStruct((stops, blocks, chunks, tc, block), f32),
        ),
        in_specs=[pl.BlockSpec(memory_space=pltpu.SMEM)] + [vmem] * 5,
        out_specs=(vmem, vmem),
        scratch_shapes=[
            pltpu.VMEM((stops + 1, chunks, tc, people), f32),
            pltpu.VMEM((chunks, 2, quads, rows + sq_rows, lanes), f32),
            pltpu.VMEM((chunks, quads, rows + sq_rows, lanes), f32),
            pltpu.VMEM((chunks, quads, rows + sq_rows, lanes), f32),
            pltpu.VMEM((chunks, 2, quads, rows + sq_rows, lanes), f32),
            pltpu.VMEM((tc, block), jnp.bfloat16),
            pltpu.VMEM((chunks, blocks, tc, block), f32),
            dma((chunks,)),
            dma((chunks,)),
            dma((chunks, quads)),
            dma((chunks, quads)),
            dma((chunks, quads)),
            dma((chunks, 2, quads)),
            dma((chunks, quads)),
            dma((stops, chunks)),
            dma((stops, chunks)),
        ],
        compiler_params=pltpu.CompilerParams(
            collective_id=0, has_side_effects=True, vmem_limit_bytes=56 * 1024 * 1024
        ),
    )(visit_order, geno, resid, posterior_inverse, droot, noise)
    after = after.reshape(traits, people).T
    changes = changes.reshape(stops, blocks, traits, block).transpose(0, 1, 3, 2)
    return after, changes.reshape(stops, blocks * block, traits)


def solution(mesh):
    in_specs = (
        P(("ind", "chip"), "mark"),
        P(("ind", "chip"), "mark"),
        P("mark", None, None),
        P(None, "mark", None),
        P(None, "mark", None),
    )
    out_specs = (P(("ind", "chip"), "mark"), P(None, "mark", None))
    shape = (mesh.shape["ind"], mesh.shape["mark"], mesh.shape["chip"])
    return jax.shard_map(
        functools.partial(local, shape), mesh=mesh, in_specs=in_specs, out_specs=out_specs, check_vma=False
    )
```

time: 639 us -> 236 us (0.37)
  waiting for transfers between devices: 285 us -> 0 us
  Pallas kernels: 0 us -> 179 us
  blocking collectives: 103 us -> 0 us
  local copies, waits for them, and re-layouts: 145 us -> 56.2 us
  matrix products: 56.6 us -> 0 us
  between operations: 33.9 us -> 0.66 us
    psum x8 -> x0, waiting for transfers between devices: 194 us -> none  [local(): scores, total_sq = lax.psum((partial_value, sq_part), ('ind', 'chip'))]
    pallas_call x0 -> x1, Pallas kernels: none -> 179 us  [local(): pl.pallas_call(functools.partial(kernel, cfg), out_shape=(jax.ShapeDtypeS...]
    gather x8 -> x1, local copies, waits for them, and re-layouts: 122 us -> 13.1 us  [local(): jnp.diagonal(posterior_inverse, axis1=1, axis2=2).astype(f32)]
    psum x8 -> x0, blocking collectives: 103 us -> none  [local(): scores, total_sq = lax.psum((partial_value, sq_part), ('ind', 'chip'))]
    ppermute x4 -> x0, waiting for transfers between devices: 91 us -> none  [from_behind(): lax.ppermute(array, axis, [(i, (i + by) % peers) for i in range(peers)])]
    dot_general x24 -> x0, matrix products: 56.6 us -> none  [the longest x8 26.1 us: posterior_step(): mean_part = jnp.dot(inverse, scaled, preferred_element_type=jnp.float32)]
    reshape x0 -> x3, local copies, waits for them, and re-layouts: none -> 15.1 us  [the longest x1 6.27 us: local(): geno = genotypes.reshape(people, blocks, block).transpose(1, 0, 2)]
    squeeze x1 -> x0, local copies, waits for them, and re-layouts: 12 us -> none  [local(): lax.dynamic_index_in_dim(posterior_inverse, local_blk, 0, keepdims=False)]
  transfers between devices with their start and end apart: 12 -> 0, of which waited for: 12 -> 0; matrix products, arithmetic and copies ran while one was open for 22% -> 0% of each run, Pallas kernels for 0% -> 0%
where the time goes in v1:
time: 236 us
  Pallas kernels  179 us (76%)
  local copies, waits for them, and re-layouts  56.2 us (24%)
    pallas_call x1, Pallas kernels, local(): pl.pallas_call(functools.partial(kernel, cfg), out_shape=(jax.ShapeDtypeS...  179 us
    unnamed x3, local copies, waits for them, and re-layouts  16.2 us
    gather x1, local copies, waits for them, and re-layouts, local(): jnp.diagonal(posterior_inverse, axis1=1, axis2=2).astype(f32)  13.1 us
    transpose x1, local copies, waits for them, and re-layouts, local(): changes.reshape(stops, blocks, traits, block).transpose(0, 1, 3, 2)  8.67 us
    reshape x1, local copies, waits for them, and re-layouts, local(): geno = genotypes.reshape(people, blocks, block).transpose(1, 0, 2)  6.27 us
    reshape x1, local copies, waits for them, and re-layouts, local(): gibbs_noise.reshape(stops, blocks, block, traits).transpose(0, 1, 3, 2)  6.25 us

profile of v1, /device:TPU:0, one launch (start us, length us, event | category | flops | bytes accessed | tf_op | source)
XLA Modules:
  0.0 235.6 jit_solution(14447250097275418403)
XLA Ops:
  0.6 1.3 copy.18.order_ref
  2.0 2.5 %copy.15 = f32[256,1024]{1,0:T(8,128)} copy(f32[256,1024]{0,1:T(8,128)} %bitcast.25) | data formatting | bytes 2097152 | tf_op jit(solution)/shard_map/transpose | solution.py:232
  4.5 6.4 %copy.13 = bf16[1024,2048]{0,1:T(8,128)(2,1)} copy(bf16[1024,2048]{1,0:T(8,128)(2,1)} %param.5) | data formatting | bytes 8388608 | tf_op args[0]
  10.9 6.3 %copy.14 = bf16[1024,2,1024]{2,0,1:T(8,128)(2,1)} copy(bf16[1024,2,1024]{0,2,1:T(8,128)(2,1)} %bitcast.20) | data formatting | bytes 8388608 | tf_op jit(solution)/shard_map/reshape | solution.py:231
  17.2 6.3 %copy.17 = bf16[4,2,1024,256]{2,3,1,0:T(8,128)(2,1)} copy(bf16[4,2,1024,256]{3,2,1,0:T(8,128)(2,1)} %bitcast.24) | data formatting | bytes 8388608 | tf_op jit(solution)/shard_map/reshape | solution.py:233
  23.4 8.5 %copy.16 = bf16[2,1024,1024]{2,0,1:T(2,128)(2,1)} copy(bf16[2,1024,1024]{2,1,0:T(8,128)(2,1)} %inv_ref.1) | data formatting | bytes 8388608 | tf_op args[2]
  31.9 13.1 %gather_fusion = bf16[1024,2]{0,1:T(2,128)(2,1)S(1)} fusion(bf16[2,1024,1024]{2,0,1:T(2,128)(2,1)} %copy.16, s32[1024]{0:T(1024)S(1)} %bitcast.17), kind=kCustom, calls=%fused_computation | custom fusion | bytes 16384 | tf_op jit(solution)/shard_map/jit(diagonal)/gather | solution.py:235
  45.1 0.6 sqrt.14.droot_ref
  45.7 178.7 %shard_map.68 = (f32[4,64,1024]{2,1,0:T(8,128)}, f32[4,2,4,64,1024]{4,3,2,1,0:T(8,128)}) custom-call(s32[4,1,2]{2,1,0:T(1,128)} %copy.18.order_ref, bf16[2,1024,1024]{2,1,0:T(8,128)(2,1)} %bitcast.18, f32[4,64,1024]{2,1,0:T(8,128)} %bitcast.23, bf16[2,1024,1024]{2,1,0:T(8,128)(2,1)} %inv_ref.1, f32[2,1,1024]{2,1,0:T(1,128)} %sqrt.14.droot_ref, ...), custom_call_target="tpu_custom_call" | custom-call | tf_op jit(solution)/shard_map/pallas_call | solution.py:239
  224.4 2.5 %copy.19 = f32[256,1024]{0,1:T(8,128)} copy(f32[256,1024]{1,0:T(8,128)} %bitcast.27) | data formatting | bytes 2097152 | tf_op jit(solution)/shard_map/reshape | solution.py:269
  226.9 8.7 %copy.20 = f32[4,2,1024,256]{3,2,1,0:T(8,128)} copy(f32[4,2,1024,256]{2,3,1,0:T(8,128)} %bitcast.21) | data formatting | bytes 16777216 | tf_op jit(solution)/shard_map/transpose | solution.py:270
  (2 shorter events, 0.0 us)

commit v2 on v1

--- a/solution.py
+++ b/solution.py
@@ -16,12 +16,18 @@
 def kernel(
     cfg,
     order_ref,
+    geno_hbm,
+    resid_hbm,
+    inv_hbm,
+    noise_hbm,
+    after_hbm,
+    change_hbm,
     geno_ref,
     resid_ref,
     inv_ref,
+    noise_raw,
+    noise_ref,
     droot_ref,
-    noise_ref,
-    after_ref,
     change_ref,
     ebuf,
     part,
@@ -30,6 +36,9 @@
     full,
     scaled,
     stash,
+    in_sem,
+    out_sem,
+    after_sem,
     p1s,
     p1r,
     p2s,
@@ -59,6 +68,21 @@
         qq = lax.rem(q + r, quads)
         return qq, {"ind": lax.div(qq, n_chip) * 2 + core, "chip": lax.rem(qq, n_chip)}
 
+    blocks = geno_ref.shape[0]
+    per_visit = chunks // blocks
+    piece = noise_ref.shape[3]
+    loads = [pltpu.make_async_copy(resid_hbm, resid_ref, in_sem.at[0])]
+    for k in range(blocks):
+        loads.append(
+            pltpu.make_async_copy(
+                geno_hbm.at[:, k * block : (k + 1) * block], geno_ref.at[k], in_sem.at[1 + k]
+            )
+        )
+    loads.append(pltpu.make_async_copy(noise_hbm, noise_raw, in_sem.at[1 + blocks]))
+    loads.append(pltpu.make_async_copy(inv_hbm, inv_ref, in_sem.at[2 + blocks]))
+    for load in loads:
+        load.start()
+
     barrier = pltpu.get_barrier_semaphore()
     pl.semaphore_signal(barrier, inc=1, device_id=partner, device_id_type=MESH)
     pl.semaphore_signal(barrier, inc=1, device_id=nxt, device_id_type=MESH)
@@ -66,8 +90,12 @@
     for r in range(1, quads):
         pl.semaphore_signal(barrier, inc=1, device_id=chip_at(r)[1], device_id_type=MESH)
 
+    loads[0].wait()
+    flipped = resid_ref[...].T
     for c in range(chunks):
-        ebuf[0, c] = resid_ref[c]
+        ebuf[0, c] = flipped[c * tc : (c + 1) * tc]
+    for k in range(blocks):
+        loads[1 + k].wait()
     pl.semaphore_wait(barrier, quads + 2)
 
     def copy(src, dst, ssem, rsem, dev):
@@ -169,7 +197,14 @@
         spread = jnp.sum(sq, axis=1, keepdims=True) * (1.0 / count)
         root = jnp.sqrt((spread + epsilon) * (1.0 / count))
         mean = lax.dot_general(scaled[...], inv_ref[k], NT, preferred_element_type=jnp.float32)
-        change = mean + (root * droot_ref[k]) * noise_ref[stop, j, c].astype(jnp.float32)
+        noise = jnp.concatenate(
+            [
+                noise_ref[stop, j * per_visit + i, pl.ds(pl.multiple_of(c * tc, tc), tc), :]
+                for i in range(per_visit)
+            ],
+            axis=1,
+        ).astype(jnp.float32)
+        change = mean + (root * droot_ref[k]) * noise
         if j == 0:
             stash[c, 0] = change
         else:
@@ -188,9 +223,29 @@
         def _():
             fn(lax.div(x, chunks), lax.rem(x, chunks))
 
+    def out_copy(stop, c):
+        return pltpu.make_async_copy(change_ref.at[stop, :, c], change_hbm.at[stop, :, c], out_sem.at[stop, c])
+
     def last(stop, c):
         phase_e(stop, 1, c)
         hop(stop, c).start()
+        out_copy(stop, c).start()
+
+    def flip(stop, i):
+        noise_ref[stop, i] = noise_raw[stop, pl.ds(pl.multiple_of(i * piece, piece), piece), :].T
+
+    def prepare():
+        loads[1 + blocks].wait()
+        lax.fori_loop(0, chunks, lambda i, x: (flip(0, i), x)[1], 0)
+        loads[2 + blocks].wait()
+        eye = lax.broadcasted_iota(jnp.int32, (128, 128), 0) == lax.broadcasted_iota(
+            jnp.int32, (128, 128), 1
+        )
+        for k in range(blocks):
+            for i in range(0, block, 128):
+                tile = inv_ref[k, i : i + 128, i : i + 128].astype(jnp.float32)
+                diag = jnp.sum(jnp.where(eye, tile, 0.0), axis=0, keepdims=True)
+                droot_ref[k, :, i : i + 128] = jnp.sqrt(diag)
 
     def middle(stop, c):
         phase_e(stop, 0, c)
@@ -201,7 +256,9 @@
         at(t, phase_a)
         at(t - 1, phase_d)
         at(t - 2, phase_c)
+        pl.when(t == 0)(prepare)
         at(t, phase_b)
+        at(t + chunks, flip)
         at(t - 1, middle)
         at(t - 2, phase_d)
         at(t, phase_c)
@@ -209,9 +266,16 @@
         return carry
 
     lax.fori_loop(0, total + 3, body, 0)
+    def finish(c):
+        return pltpu.make_async_copy(ebuf.at[stops, c], after_hbm.at[c], after_sem.at[c])
+
     for c in range(chunks):
         hop(stops - 1, c).wait()
-        after_ref[c] = ebuf[stops, c]
+        finish(c).start()
+    for c in range(chunks):
+        for stop in range(stops):
+            out_copy(stop, c).wait()
+        finish(c).wait()
 
 
 def local(mesh_shape, genotypes, residual, posterior_inverse, gibbs_noise, visit_order):
@@ -228,13 +292,8 @@
     rows = tc * (block // lanes) // slices
     sq_rows = max(8, tc // slices)
     f32 = jnp.float32
-    geno = genotypes.reshape(people, blocks, block).transpose(1, 0, 2)
-    resid = residual.T.reshape(chunks, tc, people)
-    noise = gibbs_noise.reshape(stops, blocks, block, traits).transpose(0, 1, 3, 2)
-    noise = noise.reshape(stops, blocks, chunks, tc, block)
-    droot = jnp.sqrt(jnp.diagonal(posterior_inverse, axis1=1, axis2=2).astype(f32))[:, None, :]
     cfg = (n_ind, n_mark, n_chip, chunks, stops, count, block, rows, lanes, sq_rows)
-    vmem = pl.BlockSpec(memory_space=pltpu.VMEM)
+    hbm = pl.BlockSpec(memory_space=pl.ANY)
     dma = pltpu.SemaphoreType.DMA
     after, changes = pl.pallas_call(
         functools.partial(kernel, cfg),
@@ -242,9 +301,16 @@
             jax.ShapeDtypeStruct((chunks, tc, people), f32),
             jax.ShapeDtypeStruct((stops, blocks, chunks, tc, block), f32),
         ),
-        in_specs=[pl.BlockSpec(memory_space=pltpu.SMEM)] + [vmem] * 5,
-        out_specs=(vmem, vmem),
+        in_specs=[pl.BlockSpec(memory_space=pltpu.SMEM)] + [hbm] * 4,
+        out_specs=(hbm, hbm),
         scratch_shapes=[
+            pltpu.VMEM((blocks, people, block), jnp.bfloat16),
+            pltpu.VMEM((people, traits), f32),
+            pltpu.VMEM((blocks, block, block), jnp.bfloat16),
+            pltpu.VMEM((stops, blocks * block, traits), jnp.bfloat16),
+            pltpu.VMEM((stops, chunks, traits, blocks * block // chunks), jnp.bfloat16),
+            pltpu.VMEM((blocks, 1, block), f32),
+            pltpu.VMEM((stops, blocks, chunks, tc, block), f32),
             pltpu.VMEM((stops + 1, chunks, tc, people), f32),
             pltpu.VMEM((chunks, 2, quads, rows + sq_rows, lanes), f32),
             pltpu.VMEM((chunks, quads, rows + sq_rows, lanes), f32),
@@ -252,6 +318,9 @@
             pltpu.VMEM((chunks, 2, quads, rows + sq_rows, lanes), f32),
             pltpu.VMEM((tc, block), jnp.bfloat16),
             pltpu.VMEM((chunks, blocks, tc, block), f32),
+            dma((3 + blocks,)),
+            dma((stops, chunks)),
+            dma((chunks,)),
             dma((chunks,)),
             dma((chunks,)),
             dma((chunks, quads)),
@@ -265,7 +334,7 @@
         compiler_params=pltpu.CompilerParams(
             collective_id=0, has_side_effects=True, vmem_limit_bytes=56 * 1024 * 1024
         ),
-    )(visit_order, geno, resid, posterior_inverse, droot, noise)
+    )(visit_order, genotypes, residual, posterior_inverse, gibbs_noise)
     after = after.reshape(traits, people).T
     changes = changes.reshape(stops, blocks, traits, block).transpose(0, 1, 3, 2)
     return after, changes.reshape(stops, blocks * block, traits)

time: 236 us -> 188 us (0.80)
  local copies, waits for them, and re-layouts: 56.2 us -> 12.5 us
  Pallas kernels: 179 us -> 174 us
    unnamed x3 -> x1, local copies, waits for them, and re-layouts: 16.2 us -> 1.34 us
    gather x1 -> x0, local copies, waits for them, and re-layouts: 13.1 us -> none  [local(): jnp.diagonal(posterior_inverse, axis1=1, axis2=2).astype(f32)]
    reshape x2 -> x0, local copies, waits for them, and re-layouts: 12.5 us -> none  [the longest x1 6.27 us: local(): geno = genotypes.reshape(people, blocks, block).transpose(1, 0, 2)]
    pallas_call x1, Pallas kernels: 179 us -> 174 us  [local(): pl.pallas_call(functools.partial(kernel, cfg), out_shape=(jax.ShapeDtypeS...]
    transpose x1 -> x0, local copies, waits for them, and re-layouts: 2.53 us -> none  [local(): resid = residual.T.reshape(chunks, tc, people)]
where the time goes in v2:
time: 188 us; the launch traced here: 187 us
  Pallas kernels  174 us (93%)
  local copies, waits for them, and re-layouts  12.5 us (7%)
    pallas_call x1, Pallas kernels, local(): pl.pallas_call(functools.partial(kernel, cfg), out_shape=(jax.ShapeDtypeS...  174 us
    transpose x1, local copies, waits for them, and re-layouts, local(): changes.reshape(stops, blocks, traits, block).transpose(0, 1, 3, 2)  8.67 us

profile of v2, /device:TPU:0, one launch (start us, length us, event | category | flops | bytes accessed | tf_op | source)
XLA Modules:
  0.0 187.3 jit_solution(17784384761708971761)
XLA Ops:
  0.6 1.3 copy.7.order_ref
  2.0 174.1 %shard_map.68 = (f32[4,64,1024]{2,1,0:T(8,128)}, f32[4,2,4,64,1024]{4,3,2,1,0:T(8,128)}) custom-call(s32[4,1,2]{2,1,0:T(1,128)} %copy.7.order_ref, bf16[1024,2048]{1,0:T(8,128)(2,1)} %geno_hbm.1, f32[1024,256]{1,0:T(8,128)} %resid_hbm.1, bf16[2,1024,1024]{2,1,0:T(8,128)(2,1)} %inv_hbm.1, bf16[4,2048,256]{2,1,0:T(8,128)(2,1)} %noise_hbm.1), custom_call_target="tpu_custom_call" | custom-call | tf_op jit(solution)/shard_map/pallas_call | solution.py:298
  176.1 2.5 %copy.8 = f32[256,1024]{0,1:T(8,128)} copy(f32[256,1024]{1,0:T(8,128)} %bitcast.9) | data formatting | bytes 2097152 | tf_op jit(solution)/shard_map/reshape | solution.py:338
  178.6 8.7 %copy.9 = f32[4,2,1024,256]{3,2,1,0:T(8,128)} copy(f32[4,2,1024,256]{2,3,1,0:T(8,128)} %bitcast.7) | data formatting | bytes 16777216 | tf_op jit(solution)/shard_map/transpose | solution.py:339

commit v3 on v2

--- a/solution.py
+++ b/solution.py
@@ -10,6 +10,18 @@
 epsilon = 1e-05
 MESH = pl.DeviceIdType.MESH
 CHUNKS = 4
+PERIOD = 6
+ORDER = (
+    ("m", 3),
+    ("c", 4),
+    ("l", 5),
+    ("d", 2),
+    ("b", 3),
+    ("a", 0),
+    ("c", 1),
+    ("d", 4),
+    ("b", 0),
+)
 NT = (((1,), (1,)), ((), ()))
 
 
@@ -64,9 +76,14 @@
     nxt = {"mark": lax.rem(mark + 1, n_mark)}
     prv = {"mark": lax.rem(mark + n_mark - 1, n_mark)}
 
+    x_chips = n_ind // 2
+    steps = [(dx, dy) for dx in range(x_chips) for dy in range(n_chip)][1:]
+    steps.sort(key=lambda d: min(d[0], x_chips - d[0]) + min(d[1], n_chip - d[1]))
+
     def chip_at(r):
-        qq = lax.rem(q + r, quads)
-        return qq, {"ind": lax.div(qq, n_chip) * 2 + core, "chip": lax.rem(qq, n_chip)}
+        xx = lax.rem(lax.div(ind, 2) + steps[r - 1][0], x_chips)
+        yy = lax.rem(y + steps[r - 1][1], n_chip)
+        return xx * n_chip + yy, {"ind": xx * 2 + core, "chip": yy}
 
     blocks = geno_ref.shape[0]
     per_visit = chunks // blocks
@@ -159,16 +176,16 @@
     def phase_b(stop, c):
         pair(c).wait()
         part[c, core] = part[c, core] + r1[c]
-        for r in range(1, quads):
+        for r in reversed(range(1, quads)):
             spread_out(c, r).start()
 
     def phase_c(stop, c):
         tot = part[c, core, q]
         for r in range(1, quads):
             arrived2(c, r).wait_recv()
-            tot = tot + r2[c, lax.rem(q + r, quads)]
+            tot = tot + r2[c, chip_at(r)[0]]
         full[c, core, q] = tot
-        for r in range(1, quads):
+        for r in reversed(range(1, quads)):
             gather(c, r).start()
         forward(c, q).start()
         for r in range(1, quads):
@@ -177,7 +194,7 @@
     def phase_d(stop, c):
         for r in range(1, quads):
             arrived3(c, r).wait_recv()
-            forward(c, lax.rem(q + r, quads)).start()
+            forward(c, chip_at(r)[0]).start()
         for r in range(1, quads):
             gather(c, r).wait_send()
 
@@ -216,12 +233,12 @@
             change.astype(jnp.bfloat16), geno_ref[k], NT, preferred_element_type=jnp.float32
         )
 
-    total = stops * chunks
-
     def at(x, fn):
-        @pl.when(jnp.logical_and(x >= 0, x < total))
+        stop, c = lax.div(x, PERIOD), lax.rem(x, PERIOD)
+
+        @pl.when((x >= 0) & (c < chunks) & (stop < stops))
         def _():
-            fn(lax.div(x, chunks), lax.rem(x, chunks))
+            fn(stop, c)
 
     def out_copy(stop, c):
         return pltpu.make_async_copy(change_ref.at[stop, :, c], change_hbm.at[stop, :, c], out_sem.at[stop, c])
@@ -251,21 +268,24 @@
         phase_e(stop, 0, c)
         score(stop, 1, c)
 
+    phases = {
+        "a": phase_a,
+        "b": phase_b,
+        "c": phase_c,
+        "d": phase_d,
+        "m": middle,
+        "l": last,
+    }
+
     def body(t, carry):
-        at(t - 3, last)
-        at(t, phase_a)
-        at(t - 1, phase_d)
-        at(t - 2, phase_c)
-        pl.when(t == 0)(prepare)
-        at(t, phase_b)
-        at(t + chunks, flip)
-        at(t - 1, middle)
-        at(t - 2, phase_d)
-        at(t, phase_c)
-        at(t - 1, phase_b)
+        for name, delay in ORDER:
+            if name == "b" and delay == 0:
+                pl.when(t == 0)(prepare)
+            at(t - delay, phases[name])
+        at(t + PERIOD, flip)
         return carry
 
-    lax.fori_loop(0, total + 3, body, 0)
+    lax.fori_loop(0, PERIOD * (stops - 1) + chunks + max(delay for _, delay in ORDER), body, 0)
     def finish(c):
         return pltpu.make_async_copy(ebuf.at[stops, c], after_hbm.at[c], after_sem.at[c])
 

time: 188 us -> 182 us (0.968)
  Pallas kernels: 174 us -> 168 us
    pallas_call x1, Pallas kernels: 174 us -> 168 us  [local(): pl.pallas_call(functools.partial(kernel, cfg), out_shape=(jax.ShapeDtypeS...]
where the time goes in v3:
time: 182 us; the launch traced here: 181 us
  Pallas kernels  168 us (92%)
  local copies, waits for them, and re-layouts  12.5 us (7%)
    pallas_call x1, Pallas kernels, local(): pl.pallas_call(functools.partial(kernel, cfg), out_shape=(jax.ShapeDtypeS...  168 us
    transpose x1, local copies, waits for them, and re-layouts, local(): changes.reshape(stops, blocks, traits, block).transpose(0, 1, 3, 2)  8.67 us

profile of v3, /device:TPU:0, one launch (start us, length us, event | category | flops | bytes accessed | tf_op | source)
XLA Modules:
  0.0 181.3 jit_solution(4194076185323199588)
XLA Ops:
  0.6 1.3 copy.7.order_ref
  2.0 168.1 %shard_map.68 = (f32[4,64,1024]{2,1,0:T(8,128)}, f32[4,2,4,64,1024]{4,3,2,1,0:T(8,128)}) custom-call(s32[4,1,2]{2,1,0:T(1,128)} %copy.7.order_ref, bf16[1024,2048]{1,0:T(8,128)(2,1)} %geno_hbm.1, f32[1024,256]{1,0:T(8,128)} %resid_hbm.1, bf16[2,1024,1024]{2,1,0:T(8,128)(2,1)} %inv_hbm.1, bf16[4,2048,256]{2,1,0:T(8,128)(2,1)} %noise_hbm.1), custom_call_target="tpu_custom_call" | custom-call | tf_op jit(solution)/shard_map/pallas_call | solution.py:318
  170.1 2.5 %copy.8 = f32[256,1024]{0,1:T(8,128)} copy(f32[256,1024]{1,0:T(8,128)} %bitcast.9) | data formatting | bytes 2097152 | tf_op jit(solution)/shard_map/reshape | solution.py:358
  172.6 8.7 %copy.9 = f32[4,2,1024,256]{3,2,1,0:T(8,128)} copy(f32[4,2,1024,256]{2,3,1,0:T(8,128)} %bitcast.7) | data formatting | bytes 16777216 | tf_op jit(solution)/shard_map/transpose | solution.py:359
